TPU v7x, 256 devices: a whole 4x4x8 slice. The times are simulated.
256 devices in a mesh: table: 16 (over x, y), dp: 8 (over z), col: 2 (over core).
Axes of the slice: x: 4, y: 4, z: 8, core: 2. Of those that a mesh axis runs over, the one named last changes fastest.
Arguments:
- table_weights: float32 [32768, 512], P('table', 'col'), may hold values from -6 to 6
- moment_first: float32 [32768, 512], P('table', 'col'), may hold values from -3 to 3
- moment_second: float32 [32768], P('table'), may hold values from 0.1 to 2
- hot_slices: int32 [16, 2], replicated, may hold values from 0 to 31, as said below
- upstream_grad: bfloat16 [131072, 512], P(('table', 'dp'), 'col'), may hold values from -20 to 20
- dedup_map: int32 [131072, 32], P(('table', 'dp')), may hold values from 0 to 4095, as said below
- unique_rows: int32 [128, 16, 256], P(('table', 'dp')), may hold values from 0 to 32767, as said below
- row_counts: int32 [128, 16], P(('table', 'dp')), may hold values from 192 to 256, as said below
Outputs:
- new_weights: float32 [32768, 512], P('table', 'col')
- new_first: float32 [32768, 512], P('table', 'col')
- new_second: float32 [32768], P('table')
Inputs may be any that keep to these rules, and one draw needn't show every extreme that they name: `hot_slices`: each row holds 2 different slice numbers below 32. `unique_rows`: for source device s and owner t, the first row_counts[s, t] entries are different rows r with physical(r) on table index t; the remaining entries are not used. `row_counts`: in every draw some owner receives 256 used slots from every source device. `dedup_map`: an entry in a row of source device s is a used slot t * 256 + k with k < row_counts[s, t].
All inputs are finite; a program needn't handle non-finite values.
Results may differ from a plain program's by a relative error of at most 0.0003.
Values sent between devices are 32-bit elements; how exact they have to be, the bound alone decides.
No kernel may reach another device: no remote copies, remote signals or barrier semaphores. Data moves between devices by JAX's collectives and lax.ppermute only.
A program may use at most 64 MiB of HBM per device.

v0:
```python
import jax
import jax.numpy as jnp
from jax import lax
from jax.sharding import PartitionSpec as P

SLICE = 64
beta_one = 0.9
beta_two = 0.99
learn_rate = 0.1
eps_value = 1e-08


def partner_2(block, axis, distance):
    count = lax.axis_size(axis)
    route = []
    for low in range(count):
        high = low | 1 << distance
        if high != low and high < count:
            route += [(low, high), (high, low)]
    return lax.ppermute(block, axis, route)


def local_targets(logical_rows, hot_slices, rows_dev):
    n_table = hot_slices.shape[0]
    row_owner = logical_rows // rows_dev
    local_row = logical_rows % rows_dev
    row_piece = local_row // SLICE
    row_offset = local_row % SLICE
    matches = hot_slices[row_owner] == row_piece[..., None]
    partner = (row_owner + n_table // 2) % n_table
    partner_piece = jnp.sum(jnp.where(matches, hot_slices[partner], 0), axis=-1)
    return jnp.where(jnp.any(matches, axis=-1), partner_piece * SLICE + row_offset, local_row)


def adam_rows(weights, first, second, gradient, squares, full_width):
    new_second = beta_two * second + (1.0 - beta_two) * (squares / full_width)
    new_first = beta_one * first + (1.0 - beta_one) * gradient
    scaled = jnp.sqrt(new_second / (1.0 - beta_two**8)) + eps_value
    new_weights = weights - learn_rate * (new_first / (1.0 - beta_one**8)) / scaled[:, None]
    return (new_weights, new_first, new_second)


def on_device(
    table_weights,
    moment_first,
    moment_second,
    hot_slices,
    upstream_grad,
    dedup_map,
    unique_rows,
    row_counts,
):
    n_table = lax.axis_size("table")
    position = lax.axis_index("table")
    rows_dev, col_width = table_weights.shape
    own_hot = hot_slices[position]
    n_hots = own_hot.shape[0]
    starts = [own_hot[k] * SLICE for k in range(n_hots)]
    out_weights = jnp.stack(
        [lax.dynamic_slice_in_dim(table_weights, starts[k], SLICE, 0) for k in range(n_hots)]
    )
    out_first = jnp.stack(
        [lax.dynamic_slice_in_dim(moment_first, starts[k], SLICE, 0) for k in range(n_hots)]
    )
    out_second = jnp.stack(
        [lax.dynamic_slice_in_dim(moment_second, starts[k], SLICE, 0) for k in range(n_hots)]
    )
    swap_bit = n_table.bit_length() - 2
    incoming = partner_2((out_weights, out_first, out_second), "table", swap_bit)
    placed_weights = table_weights
    placed_first = moment_first
    placed_second = moment_second
    for k in range(n_hots):
        placed_weights = lax.dynamic_update_slice_in_dim(
            placed_weights, incoming[0][k], starts[k], 0
        )
        placed_first = lax.dynamic_update_slice_in_dim(placed_first, incoming[1][k], starts[k], 0)
        placed_second = lax.dynamic_update_slice_in_dim(placed_second, incoming[2][k], starts[k], 0)
    slot_cap = unique_rows.shape[2]
    valid = jnp.arange(slot_cap)[None, :] < row_counts[0][:, None]
    targets = jnp.where(valid, local_targets(unique_rows[0], hot_slices, rows_dev), rows_dev)
    slot_iota = jnp.arange(slot_cap)

    def owner_block(carry, owner):
        wanted = slot_iota + owner * slot_cap
        tally = jnp.sum(
            (dedup_map[None, :, :] == wanted[:, None, None]).astype(jnp.float32), axis=2
        )
        block = jnp.dot(
            tally.astype(jnp.bfloat16), upstream_grad, preferred_element_type=jnp.float32
        )
        return (carry, block)

    _, slot_grad = lax.scan(owner_block, 0, jnp.arange(n_table))
    got_grad, got_target = (
        lax.all_to_all(slot_grad, "table", split_axis=0, concat_axis=0, tiled=True),
        lax.all_to_all(targets, "table", split_axis=0, concat_axis=0, tiled=True),
    )
    row_iota = jnp.arange(rows_dev)

    def add_source(total, inputs):
        grad_block, target_block = inputs
        select = (row_iota[:, None] == target_block[None, :]).astype(jnp.float32)
        return (
            total
            + jnp.dot(
                select,
                grad_block,
                precision=lax.Precision.HIGHEST,
                preferred_element_type=jnp.float32,
            ),
            None,
        )

    dense, _ = lax.scan(
        add_source, jnp.zeros((rows_dev, col_width), jnp.float32), (got_grad, got_target)
    )
    full_width = col_width * lax.axis_size("col")
    gradient = lax.psum(dense, "dp")
    squares = lax.psum(jnp.sum(gradient * gradient, axis=1), "col")
    new_weights, new_first, new_second = adam_rows(
        placed_weights, placed_first, placed_second, gradient, squares, full_width
    )
    return (new_weights, new_first, new_second)


def solution(mesh):
    placed = (
        P("table", "col"),
        P("table", "col"),
        P("table"),
        P(),
        P(("table", "dp"), "col"),
        P(("table", "dp"), None),
        P(("table", "dp"), None, None),
        P(("table", "dp"), None),
    )
    return jax.shard_map(
        on_device,
        mesh=mesh,
        in_specs=placed,
        out_specs=(P("table", "col"), P("table", "col"), P("table")),
        check_vma=False,
    )
```

profile of v0, /device:TPU:1, one launch (start us, length us, event | category | flops | bytes accessed | tf_op | source)
XLA Modules:
  0.0 479.1 jit_solution(15004162492710192044)
XLA Ops:
  7.2 3.2 copy.52
  10.4 1.3 copy.53
  11.9 10.8 %gather_fusion = s32[4096,2]{1,0:T(8,128)S(1)} fusion(s32[16,2]{1,0:T(8,128)S(1)} %copy.21, s32[4096]{0:T(1024)S(1)} %broadcast_clamp_fusion.1), kind=kCustom, calls=%fused_computation | custom fusion | bytes 81920 | tf_op jit(solution)/shard_map/gather | solution.py:29
  22.7 14.1 %gather_fusion.1 = s32[4096,2]{1,0:T(8,128)} fusion(s32[16,2]{1,0:T(8,128)S(1)} %copy.21, s32[4096]{0:T(1024)S(1)} %broadcast_clamp_fusion), kind=kCustom, calls=%fused_computation.1 | custom fusion | bytes 81920 | tf_op jit(solution)/shard_map/gather | solution.py:31
  36.8 1.3 fusion.29
  39.8 7.6 %all-to-all-start = ((s32[16,1,256]{2,1,0:T(1,128)}), s32[16,1,256]{2,1,0:T(1,128)S(1)}, u32[]{:S(2)}, u32[]{:S(2)}) async-start(s32[16,1,256]{2,1,0:T(1,128)} %copy.23), calls=%async_computation | async-start | bytes 32768 | tf_op jit(solution)/shard_map/all_to_all | solution.py:97
  47.4 217.9 %while.22 = (s32[]{:T(128)}, f32[16,256,256]{2,1,0:T(8,128)}, s32[1024,32]{0,1:T(8,128)S(1)}, s32[16]{0:T(128)S(1)}, bf16[1024,256]{1,0:T(8,128)(2,1)S(1)}, /*index=5*/s32[]{:T(128)}, s32[1]{0:T(128)}) while((s32[]{:T(128)}, f32[16,256,256]{2,1,0:T(8,128)}, s32[1024,32]{0,1:T(8,128)S(1)}, s32[16]{0:T(128)S(1)}, ...), condition=%wide.region_2.3_spmd.clone, body=%wide.region_0.2_spmd.clone.sunk | while | flops 159121664 | bytes 1968745 | solution.py:94
  48.9 11.3 %convert_reduce_fusion.2 = bf16[256,1024]{1,0:T(8,128)(2,1)S(1)} fusion(s32[1024,32]{0,1:T(8,128)S(1)} %get-tuple-element.201, s32[256]{0:T(256)S(1)} %iota_add_fusion.2), kind=kLoop, calls=%fused_computation.4.clone.1 | loop fusion | flops 24903680 | bytes 656384 | tf_op jit(solution)/shard_map/while/body/eval_jaxpr/reduce_sum | solution.py:86
  60.2 1.0 fusion.39
  62.5 11.3 %convert_reduce_fusion.2 = bf16[256,1024]{1,0:T(8,128)(2,1)S(1)} fusion(s32[1024,32]{0,1:T(8,128)S(1)} %get-tuple-element.201, s32[256]{0:T(256)S(1)} %iota_add_fusion.2), kind=kLoop, calls=%fused_computation.4.clone.1 | loop fusion | flops 24903680 | bytes 656384 | tf_op jit(solution)/shard_map/while/body/eval_jaxpr/reduce_sum | solution.py:86
  73.8 1.0 fusion.39
  76.1 11.3 %convert_reduce_fusion.2 = bf16[256,1024]{1,0:T(8,128)(2,1)S(1)} fusion(s32[1024,32]{0,1:T(8,128)S(1)} %get-tuple-element.201, s32[256]{0:T(256)S(1)} %iota_add_fusion.2), kind=kLoop, calls=%fused_computation.4.clone.1 | loop fusion | flops 24903680 | bytes 656384 | tf_op jit(solution)/shard_map/while/body/eval_jaxpr/reduce_sum | solution.py:86
  87.4 1.0 fusion.39
  89.7 11.3 %convert_reduce_fusion.2 = bf16[256,1024]{1,0:T(8,128)(2,1)S(1)} fusion(s32[1024,32]{0,1:T(8,128)S(1)} %get-tuple-element.201, s32[256]{0:T(256)S(1)} %iota_add_fusion.2), kind=kLoop, calls=%fused_computation.4.clone.1 | loop fusion | flops 24903680 | bytes 656384 | tf_op jit(solution)/shard_map/while/body/eval_jaxpr/reduce_sum | solution.py:86
  101.0 1.0 fusion.39
  103.3 11.3 %convert_reduce_fusion.2 = bf16[256,1024]{1,0:T(8,128)(2,1)S(1)} fusion(s32[1024,32]{0,1:T(8,128)S(1)} %get-tuple-element.201, s32[256]{0:T(256)S(1)} %iota_add_fusion.2), kind=kLoop, calls=%fused_computation.4.clone.1 | loop fusion | flops 24903680 | bytes 656384 | tf_op jit(solution)/shard_map/while/body/eval_jaxpr/reduce_sum | solution.py:86
  114.6 1.0 fusion.39
  116.9 11.3 %convert_reduce_fusion.2 = bf16[256,1024]{1,0:T(8,128)(2,1)S(1)} fusion(s32[1024,32]{0,1:T(8,128)S(1)} %get-tuple-element.201, s32[256]{0:T(256)S(1)} %iota_add_fusion.2), kind=kLoop, calls=%fused_computation.4.clone.1 | loop fusion | flops 24903680 | bytes 656384 | tf_op jit(solution)/shard_map/while/body/eval_jaxpr/reduce_sum | solution.py:86
  128.2 1.0 fusion.39
  130.5 11.3 %convert_reduce_fusion.2 = bf16[256,1024]{1,0:T(8,128)(2,1)S(1)} fusion(s32[1024,32]{0,1:T(8,128)S(1)} %get-tuple-element.201, s32[256]{0:T(256)S(1)} %iota_add_fusion.2), kind=kLoop, calls=%fused_computation.4.clone.1 | loop fusion | flops 24903680 | bytes 656384 | tf_op jit(solution)/shard_map/while/body/eval_jaxpr/reduce_sum | solution.py:86
  141.8 1.0 fusion.39
  144.1 11.3 %convert_reduce_fusion.2 = bf16[256,1024]{1,0:T(8,128)(2,1)S(1)} fusion(s32[1024,32]{0,1:T(8,128)S(1)} %get-tuple-element.201, s32[256]{0:T(256)S(1)} %iota_add_fusion.2), kind=kLoop, calls=%fused_computation.4.clone.1 | loop fusion | flops 24903680 | bytes 656384 | tf_op jit(solution)/shard_map/while/body/eval_jaxpr/reduce_sum | solution.py:86
  157.7 11.3 %convert_reduce_fusion.2 = bf16[256,1024]{1,0:T(8,128)(2,1)S(1)} fusion(s32[1024,32]{0,1:T(8,128)S(1)} %get-tuple-element.201, s32[256]{0:T(256)S(1)} %iota_add_fusion.2), kind=kLoop, calls=%fused_computation.4.clone.1 | loop fusion | flops 24903680 | bytes 656384 | tf_op jit(solution)/shard_map/while/body/eval_jaxpr/reduce_sum | solution.py:86
  169.0 1.0 fusion.39
  171.3 11.3 %convert_reduce_fusion.2 = bf16[256,1024]{1,0:T(8,128)(2,1)S(1)} fusion(s32[1024,32]{0,1:T(8,128)S(1)} %get-tuple-element.201, s32[256]{0:T(256)S(1)} %iota_add_fusion.2), kind=kLoop, calls=%fused_computation.4.clone.1 | loop fusion | flops 24903680 | bytes 656384 | tf_op jit(solution)/shard_map/while/body/eval_jaxpr/reduce_sum | solution.py:86
  182.6 1.0 fusion.39
  184.9 11.3 %convert_reduce_fusion.2 = bf16[256,1024]{1,0:T(8,128)(2,1)S(1)} fusion(s32[1024,32]{0,1:T(8,128)S(1)} %get-tuple-element.201, s32[256]{0:T(256)S(1)} %iota_add_fusion.2), kind=kLoop, calls=%fused_computation.4.clone.1 | loop fusion | flops 24903680 | bytes 656384 | tf_op jit(solution)/shard_map/while/body/eval_jaxpr/reduce_sum | solution.py:86
  196.2 1.0 fusion.39
  198.5 11.3 %convert_reduce_fusion.2 = bf16[256,1024]{1,0:T(8,128)(2,1)S(1)} fusion(s32[1024,32]{0,1:T(8,128)S(1)} %get-tuple-element.201, s32[256]{0:T(256)S(1)} %iota_add_fusion.2), kind=kLoop, calls=%fused_computation.4.clone.1 | loop fusion | flops 24903680 | bytes 656384 | tf_op jit(solution)/shard_map/while/body/eval_jaxpr/reduce_sum | solution.py:86
  209.8 1.0 fusion.39
  212.1 11.3 %convert_reduce_fusion.2 = bf16[256,1024]{1,0:T(8,128)(2,1)S(1)} fusion(s32[1024,32]{0,1:T(8,128)S(1)} %get-tuple-element.201, s32[256]{0:T(256)S(1)} %iota_add_fusion.2), kind=kLoop, calls=%fused_computation.4.clone.1 | loop fusion | flops 24903680 | bytes 656384 | tf_op jit(solution)/shard_map/while/body/eval_jaxpr/reduce_sum | solution.py:86
  225.7 11.3 %convert_reduce_fusion.2 = bf16[256,1024]{1,0:T(8,128)(2,1)S(1)} fusion(s32[1024,32]{0,1:T(8,128)S(1)} %get-tuple-element.201, s32[256]{0:T(256)S(1)} %iota_add_fusion.2), kind=kLoop, calls=%fused_computation.4.clone.1 | loop fusion | flops 24903680 | bytes 656384 | tf_op jit(solution)/shard_map/while/body/eval_jaxpr/reduce_sum | solution.py:86
  237.1 1.0 fusion.39
  239.3 11.3 %convert_reduce_fusion.2 = bf16[256,1024]{1,0:T(8,128)(2,1)S(1)} fusion(s32[1024,32]{0,1:T(8,128)S(1)} %get-tuple-element.201, s32[256]{0:T(256)S(1)} %iota_add_fusion.2), kind=kLoop, calls=%fused_computation.4.clone.1 | loop fusion | flops 24903680 | bytes 656384 | tf_op jit(solution)/shard_map/while/body/eval_jaxpr/reduce_sum | solution.py:86
  252.9 11.3 %convert_reduce_fusion.2 = bf16[256,1024]{1,0:T(8,128)(2,1)S(1)} fusion(s32[1024,32]{0,1:T(8,128)S(1)} %get-tuple-element.201, s32[256]{0:T(256)S(1)} %iota_add_fusion.2), kind=kLoop, calls=%fused_computation.4.clone.1 | loop fusion | flops 24903680 | bytes 656384 | tf_op jit(solution)/shard_map/while/body/eval_jaxpr/reduce_sum | solution.py:86
  264.2 1.0 fusion.39
  265.3 6.7 %all-to-all-start.1 = ((f32[16,256,256]{2,1,0:T(8,128)}), f32[16,256,256]{2,1,0:T(8,128)}, u32[]{:S(2)}, u32[]{:S(2)}) async-start(f32[16,256,256]{2,1,0:T(8,128)} %get-tuple-element.62), calls=%async_computation.1 | async-start | bytes 8388608 | tf_op jit(solution)/shard_map/all_to_all | solution.py:96
  272.1 51.8 %all-to-all-done.1 = f32[16,256,256]{2,1,0:T(8,128)} async-done(((f32[16,256,256]{2,1,0:T(8,128)}), f32[16,256,256]{2,1,0:T(8,128)}, u32[]{:S(2)}, u32[]{:S(2)}) %all-to-all-start.1) | async-done | bytes 4194336 | tf_op jit(solution)/shard_map/all_to_all | solution.py:96
  323.9 45.4 %while.23 = (s32[]{:T(128)}, f32[2048,256]{1,0:T(8,128)S(1)}, s32[16,256]{1,0:T(8,128)S(1)}, f32[16,256,256]{2,1,0:T(8,128)}, s32[]{:T(128)}, /*index=5*/s32[]{:T(128)}) while((s32[]{:T(128)}, f32[2048,256]{1,0:T(8,128)S(1)}, s32[16,256]{1,0:T(8,128)S(1)}, f32[16,256,256]{2,1,0:T(8,128)}, s32[]{:T(128)}, /*index=5*/s32[]{:T(128)}) %tuple.62), condition=%wide.region_6.7_spmd.clone, body=%wide.region_5.6_spmd.clone.sunk | while | flops 1612185600 | bytes 4460115 | solution.py:115
  323.9 2.8 convolution_add_fusion.2
  326.7 2.8 convolution_add_fusion.2
  329.6 2.8 convolution_add_fusion.2
  332.4 2.8 convolution_add_fusion.2
  335.2 2.8 convolution_add_fusion.2
  338.1 2.8 convolution_add_fusion.2
  340.9 2.8 convolution_add_fusion.2
  343.8 2.8 convolution_add_fusion.2
  346.6 2.8 convolution_add_fusion.2
  349.4 2.8 convolution_add_fusion.2
  352.3 2.8 convolution_add_fusion.2
  355.1 2.8 convolution_add_fusion.2
  358.0 2.8 convolution_add_fusion.2
  360.8 2.8 convolution_add_fusion.2
  363.6 2.8 convolution_add_fusion.2
  366.5 2.8 convolution_add_fusion.2
  369.3 1.3 copy-done
  373.5 4.6 collective-permute-start.1
  378.2 3.0 collective-permute-start
  381.3 1.2 collective-permute-done.2
  383.9 1.0 collective-permute-done
  386.2 73.0 %all-reduce.2.cloned.1.call-done = f32[2048,256]{1,0:T(8,128)} async-done(((f32[2048,256]{1,0:T(8,128)}), f32[2048,256]{1,0:T(8,128)}) %all-reduce.2.cloned.1.call-update) | async-done | bytes 2097168 | tf_op jit(solution)/shard_map/psum | solution.py:119
  459.1 1.9 multiply_reduce_fusion
  461.1 5.8 %psum.15 = f32[2048]{0:T(1024)S(1)} all-reduce(f32[2048]{0:T(1024)S(1)} %multiply_reduce_fusion), channel_id=1, replica_groups=mesh['table'=16,'dp'=8,'col'=2] {'col'}, use_global_device_ids=true, to_apply=%region_9.10 | all-reduce | flops 2048 | bytes 16384 | tf_op jit(solution)/shard_map/psum | solution.py:120
  467.5 4.8 divide_subtract_fusion
  (104 shorter events, 19.9 us)
Async XLA Ops:
  7.2 3.2 copy-start.5
  10.4 1.3 copy-start.7
  10.4 1.3 copy-start.6
  10.4 1.4 copy-start.8
  36.8 1.6 copy-start.3
  36.8 2.3 copy-start.9
  36.8 10.6 %copy-start.1 = (bf16[1024,256]{1,0:T(8,128)(2,1)S(1)}, bf16[1024,256]{1,0:T(8,128)(2,1)}, u32[]{:S(2)}) copy-start(bf16[1024,256]{1,0:T(8,128)(2,1)} %param.16) | copy-start | bytes 1572868
  36.8 10.6 %copy-start.4 = (s32[1024,32]{0,1:T(8,128)S(1)}, s32[1024,32]{0,1:T(8,128)}, u32[]{:S(2)}) copy-start(s32[1024,32]{0,1:T(8,128)} %param.17) | copy-start | bytes 393220
  39.8 225.5 %all-to-all-start = ((s32[16,1,256]{2,1,0:T(1,128)}), s32[16,1,256]{2,1,0:T(1,128)S(1)}, u32[]{:S(2)}, u32[]{:S(2)}) async-start(s32[16,1,256]{2,1,0:T(1,128)} %copy.23), calls=%async_computation | async-start | bytes 32768 | tf_op jit(solution)/shard_map/all_to_all | solution.py:97
  265.3 58.6 %all-to-all-start.1 = ((f32[16,256,256]{2,1,0:T(8,128)}), f32[16,256,256]{2,1,0:T(8,128)}, u32[]{:S(2)}, u32[]{:S(2)}) async-start(f32[16,256,256]{2,1,0:T(8,128)} %get-tuple-element.62), calls=%async_computation.1 | async-start | bytes 8388608 | tf_op jit(solution)/shard_map/all_to_all | solution.py:96
  272.0 187.1 %all-reduce.2.cloned.1.call-start = ((), (), s32[]{:S(2)}) async-start(), calls=%async_computation.2 | async-start | bytes 4194304 | tf_op jit(solution)/shard_map/psum | solution.py:119
  369.3 1.3 copy-start
  373.5 9.1 %collective-permute-start.1 = (f32[2,64,256]{2,1,0:T(8,128)S(1)}, f32[2,64,256]{2,1,0:T(8,128)S(1)}, u32[]{:S(2)}, u32[]{:S(2)}) collective-permute-start(f32[2,64,256]{2,1,0:T(8,128)S(1)} %pad_maximum_fusion.1), channel_id=1, source_target_pairs={{0,128},{128,0},{16,144},{144,16},{32,160},{160,32},{48,176},{176,... | collective-permute-start | bytes 393224 | tf_op jit(solution)/shard_map/ppermute | solution.py:20
  378.1 4.3 collective-permute-start.2
  378.2 6.7 %collective-permute-start = (f32[2,64,256]{2,1,0:T(8,128)S(1)}, f32[2,64,256]{2,1,0:T(8,128)S(1)}, u32[]{:S(2)}, u32[]{:S(2)}) collective-permute-start(f32[2,64,256]{2,1,0:T(8,128)S(1)} %pad_maximum_fusion), channel_id=1, source_target_pairs={{0,128},{128,0},{16,144},{144,16},{32,160},{160,32},{48,176},{176,... | collective-permute-start | bytes 393224 | tf_op jit(solution)/shard_map/ppermute | solution.py:20
  386.2 81.4 %copy-start.2 = (f32[2048,256]{1,0:T(8,128)S(1)}, f32[2048,256]{1,0:T(8,128)}, u32[]{:S(2)}) copy-start(f32[2048,256]{1,0:T(8,128)} %fusion.12) | copy-start | bytes 6291460
Sparse Core Ops, SparseCore 0:
  370.8 88.3 all-reduce.1
where the time goes:
time: 480 us; the launch traced here: 479 us
  other arithmetic  191 us (40%)
  waiting for transfers between devices  127 us (26%)
  matrix products  60.9 us (13%)
  local copies, waits for them, and re-layouts  45.9 us (10%)
  starting transfers between devices  22 us (5%)
  between operations  15.5 us (3%)
  loops' own time  11.2 us (2%)
  blocking collectives  5.83 us (1%)
    reduce_sum x16, other arithmetic, owner_block(): jnp.sum((dedup_map[None, :, :] == wanted[:, None, None]).astype(jnp.float...  181 us
    psum x1, waiting for transfers between devices, on_device(): gradient = lax.psum(dense, 'dp')  73 us
    all_to_all x1, waiting for transfers between devices, on_device(): lax.all_to_all(slot_grad, 'table', split_axis=0, concat_axis=0, tiled=True)  51.8 us
    dot_general x16, matrix products, add_source(): jnp.dot(select, grad_block, precision=lax.Precision.HIGHEST, preferred_el...  44.7 us
    dot_general x16, matrix products, owner_block(): jnp.dot(tally.astype(jnp.bfloat16), upstream_grad, preferred_element_type...  16.2 us
    gather x1, local copies, waits for them, and re-layouts, local_targets(): partner_piece = jnp.sum(jnp.where(matches, hot_slices[partner], 0), axis=-1)  14.1 us
    gather x1, local copies, waits for them, and re-layouts, local_targets(): matches = hot_slices[row_owner] == row_piece[..., None]  10.8 us
    another operation x1, loops' own time, on_device(): _, slot_grad = lax.scan(owner_block, 0, jnp.arange(n_table))  10.7 us
  transfers between devices with their start and end apart: 6, of which 4 were waited for; matrix products, arithmetic and copies ran while one was open for 44% of the time, Pallas kernels for 0%

commit v1 on v0

--- a/solution.py
+++ b/solution.py
@@ -1,13 +1,30 @@
+import functools
 import jax
 import jax.numpy as jnp
 from jax import lax
 from jax.sharding import PartitionSpec as P
+from jax.lax import axis_size, ppermute
 
 SLICE = 64
 beta_one = 0.9
 beta_two = 0.99
 learn_rate = 0.1
 eps_value = 1e-08
+
+
+def feed_sites_all(q_in, comm_axis):
+    amount_of = axis_size(comm_axis)
+    piece_now, parts_out = (q_in, 0)
+    while 1 << parts_out < amount_of:
+        local_next = ppermute(
+            piece_now, comm_axis, [(hop_no, hop_no ^ 1 << parts_out) for hop_no in range(amount_of)]
+        )
+        piece_now = piece_now + local_next
+        parts_out = parts_out + 1
+    return piece_now
+
+
+assign_the_rates = functools.partial(feed_sites_all, comm_axis="dp")
 
 
 def partner_2(block, axis, distance):
@@ -116,7 +133,7 @@
         add_source, jnp.zeros((rows_dev, col_width), jnp.float32), (got_grad, got_target)
     )
     full_width = col_width * lax.axis_size("col")
-    gradient = lax.psum(dense, "dp")
+    gradient = assign_the_rates(dense)
     squares = lax.psum(jnp.sum(gradient * gradient, axis=1), "col")
     new_weights, new_first, new_second = adam_rows(
         placed_weights, placed_first, placed_second, gradient, squares, full_width

time: 480 us -> 619 us (1.29)
  waiting for transfers between devices: 127 us -> 258 us
  starting transfers between devices: 22 us -> 36.2 us
  between operations: 15.5 us -> 2.16 us
    ppermute x0 -> x3, waiting for transfers between devices: none -> 203 us  [feed_sites_all(): ppermute(piece_now, comm_axis, [(hop_no, hop_no ^ 1 << parts_out) for hop...]
    psum x1 -> x0, waiting for transfers between devices: 73 us -> none  [on_device(): gradient = lax.psum(dense, 'dp')]
    ppermute x0 -> x3, starting transfers between devices: none -> 11.4 us  [feed_sites_all(): ppermute(piece_now, comm_axis, [(hop_no, hop_no ^ 1 << parts_out) for hop...]
  transfers between devices with their start and end apart: 6 -> 8, of which waited for: 4 -> 6; matrix products, arithmetic and copies ran while one was open for 44% -> 35% of each run, Pallas kernels for 0% -> 0%
where the time goes in v1:
time: 619 us; the launch traced here: 613 us
  waiting for transfers between devices  258 us (42%)
  other arithmetic  196 us (32%)
  matrix products  60.9 us (10%)
  local copies, waits for them, and re-layouts  45.3 us (7%)
  starting transfers between devices  36.2 us (6%)
  loops' own time  11 us (2%)
    ppermute x3, waiting for transfers between devices, feed_sites_all(): ppermute(piece_now, comm_axis, [(hop_no, hop_no ^ 1 << parts_out) for hop...  203 us
    reduce_sum x16, other arithmetic, owner_block(): jnp.sum((dedup_map[None, :, :] == wanted[:, None, None]).astype(jnp.float...  181 us
    all_to_all x1, waiting for transfers between devices, on_device(): lax.all_to_all(slot_grad, 'table', split_axis=0, concat_axis=0, tiled=True)  51.8 us
    dot_general x16, matrix products, add_source(): jnp.dot(select, grad_block, precision=lax.Precision.HIGHEST, preferred_el...  44.7 us
    dot_general x16, matrix products, owner_block(): jnp.dot(tally.astype(jnp.bfloat16), upstream_grad, preferred_element_type...  16.2 us
    gather x1, local copies, waits for them, and re-layouts, local_targets(): partner_piece = jnp.sum(jnp.where(matches, hot_slices[partner], 0), axis=-1)  14.1 us
  transfers between devices with their start and end apart: 8, of which 6 were waited for; matrix products, arithmetic and copies ran while one was open for 35% of the time, Pallas kernels for 0%

profile of v1, /device:TPU:1, one launch (start us, length us, event | category | flops | bytes accessed | tf_op | source)
XLA Modules:
  0.0 613.0 jit_solution(1509271776461202597)
XLA Ops:
  1.3 3.2 copy.51
  4.5 1.3 copy.52
  6.1 10.8 %gather_fusion = s32[4096,2]{1,0:T(8,128)S(1)} fusion(s32[16,2]{1,0:T(8,128)S(1)} %copy.21, s32[4096]{0:T(1024)S(1)} %broadcast_clamp_fusion.1), kind=kCustom, calls=%fused_computation | custom fusion | bytes 81920 | tf_op jit(solution)/shard_map/gather | solution.py:46
  16.8 14.1 %gather_fusion.1 = s32[4096,2]{1,0:T(8,128)} fusion(s32[16,2]{1,0:T(8,128)S(1)} %copy.21, s32[4096]{0:T(1024)S(1)} %broadcast_clamp_fusion), kind=kCustom, calls=%fused_computation.1 | custom fusion | bytes 81920 | tf_op jit(solution)/shard_map/gather | solution.py:48
  30.9 1.3 fusion.29
  33.9 7.6 %all-to-all-start = ((s32[16,1,256]{2,1,0:T(1,128)}), s32[16,1,256]{2,1,0:T(1,128)S(1)}, u32[]{:S(2)}, u32[]{:S(2)}) async-start(s32[16,1,256]{2,1,0:T(1,128)} %copy.23), calls=%async_computation | async-start | bytes 32768 | tf_op jit(solution)/shard_map/all_to_all | solution.py:114
  41.6 217.7 %while.22 = (s32[]{:T(128)}, f32[16,256,256]{2,1,0:T(8,128)}, s32[1024,32]{0,1:T(8,128)S(1)}, s32[16]{0:T(128)S(1)}, bf16[1024,256]{1,0:T(8,128)(2,1)S(1)}, /*index=5*/s32[]{:T(128)}, s32[1]{0:T(128)}) while((s32[]{:T(128)}, f32[16,256,256]{2,1,0:T(8,128)}, s32[1024,32]{0,1:T(8,128)S(1)}, s32[16]{0:T(128)S(1)}, ...), condition=%wide.region_2.3_spmd.clone, body=%wide.region_0.2_spmd.clone.sunk | while | flops 159121664 | bytes 1968745 | solution.py:111
  42.8 11.3 %convert_reduce_fusion.2 = bf16[256,1024]{1,0:T(8,128)(2,1)S(1)} fusion(s32[1024,32]{0,1:T(8,128)S(1)} %get-tuple-element.201, s32[256]{0:T(256)S(1)} %iota_add_fusion.2), kind=kLoop, calls=%fused_computation.4.clone.1 | loop fusion | flops 24903680 | bytes 656384 | tf_op jit(solution)/shard_map/while/body/eval_jaxpr/reduce_sum | solution.py:103
  54.2 1.0 fusion.39
  56.4 11.3 %convert_reduce_fusion.2 = bf16[256,1024]{1,0:T(8,128)(2,1)S(1)} fusion(s32[1024,32]{0,1:T(8,128)S(1)} %get-tuple-element.201, s32[256]{0:T(256)S(1)} %iota_add_fusion.2), kind=kLoop, calls=%fused_computation.4.clone.1 | loop fusion | flops 24903680 | bytes 656384 | tf_op jit(solution)/shard_map/while/body/eval_jaxpr/reduce_sum | solution.py:103
  67.8 1.0 fusion.39
  70.1 11.3 %convert_reduce_fusion.2 = bf16[256,1024]{1,0:T(8,128)(2,1)S(1)} fusion(s32[1024,32]{0,1:T(8,128)S(1)} %get-tuple-element.201, s32[256]{0:T(256)S(1)} %iota_add_fusion.2), kind=kLoop, calls=%fused_computation.4.clone.1 | loop fusion | flops 24903680 | bytes 656384 | tf_op jit(solution)/shard_map/while/body/eval_jaxpr/reduce_sum | solution.py:103
  81.4 1.0 fusion.39
  83.7 11.3 %convert_reduce_fusion.2 = bf16[256,1024]{1,0:T(8,128)(2,1)S(1)} fusion(s32[1024,32]{0,1:T(8,128)S(1)} %get-tuple-element.201, s32[256]{0:T(256)S(1)} %iota_add_fusion.2), kind=kLoop, calls=%fused_computation.4.clone.1 | loop fusion | flops 24903680 | bytes 656384 | tf_op jit(solution)/shard_map/while/body/eval_jaxpr/reduce_sum | solution.py:103
  97.3 11.3 %convert_reduce_fusion.2 = bf16[256,1024]{1,0:T(8,128)(2,1)S(1)} fusion(s32[1024,32]{0,1:T(8,128)S(1)} %get-tuple-element.201, s32[256]{0:T(256)S(1)} %iota_add_fusion.2), kind=kLoop, calls=%fused_computation.4.clone.1 | loop fusion | flops 24903680 | bytes 656384 | tf_op jit(solution)/shard_map/while/body/eval_jaxpr/reduce_sum | solution.py:103
  108.6 1.0 fusion.39
  110.9 11.3 %convert_reduce_fusion.2 = bf16[256,1024]{1,0:T(8,128)(2,1)S(1)} fusion(s32[1024,32]{0,1:T(8,128)S(1)} %get-tuple-element.201, s32[256]{0:T(256)S(1)} %iota_add_fusion.2), kind=kLoop, calls=%fused_computation.4.clone.1 | loop fusion | flops 24903680 | bytes 656384 | tf_op jit(solution)/shard_map/while/body/eval_jaxpr/reduce_sum | solution.py:103
  122.2 1.0 fusion.39
  124.5 11.3 %convert_reduce_fusion.2 = bf16[256,1024]{1,0:T(8,128)(2,1)S(1)} fusion(s32[1024,32]{0,1:T(8,128)S(1)} %get-tuple-element.201, s32[256]{0:T(256)S(1)} %iota_add_fusion.2), kind=kLoop, calls=%fused_computation.4.clone.1 | loop fusion | flops 24903680 | bytes 656384 | tf_op jit(solution)/shard_map/while/body/eval_jaxpr/reduce_sum | solution.py:103
  135.8 1.0 fusion.39
  138.1 11.3 %convert_reduce_fusion.2 = bf16[256,1024]{1,0:T(8,128)(2,1)S(1)} fusion(s32[1024,32]{0,1:T(8,128)S(1)} %get-tuple-element.201, s32[256]{0:T(256)S(1)} %iota_add_fusion.2), kind=kLoop, calls=%fused_computation.4.clone.1 | loop fusion | flops 24903680 | bytes 656384 | tf_op jit(solution)/shard_map/while/body/eval_jaxpr/reduce_sum | solution.py:103
  151.7 11.3 %convert_reduce_fusion.2 = bf16[256,1024]{1,0:T(8,128)(2,1)S(1)} fusion(s32[1024,32]{0,1:T(8,128)S(1)} %get-tuple-element.201, s32[256]{0:T(256)S(1)} %iota_add_fusion.2), kind=kLoop, calls=%fused_computation.4.clone.1 | loop fusion | flops 24903680 | bytes 656384 | tf_op jit(solution)/shard_map/while/body/eval_jaxpr/reduce_sum | solution.py:103
  165.3 11.3 %convert_reduce_fusion.2 = bf16[256,1024]{1,0:T(8,128)(2,1)S(1)} fusion(s32[1024,32]{0,1:T(8,128)S(1)} %get-tuple-element.201, s32[256]{0:T(256)S(1)} %iota_add_fusion.2), kind=kLoop, calls=%fused_computation.4.clone.1 | loop fusion | flops 24903680 | bytes 656384 | tf_op jit(solution)/shard_map/while/body/eval_jaxpr/reduce_sum | solution.py:103
  178.9 11.3 %convert_reduce_fusion.2 = bf16[256,1024]{1,0:T(8,128)(2,1)S(1)} fusion(s32[1024,32]{0,1:T(8,128)S(1)} %get-tuple-element.201, s32[256]{0:T(256)S(1)} %iota_add_fusion.2), kind=kLoop, calls=%fused_computation.4.clone.1 | loop fusion | flops 24903680 | bytes 656384 | tf_op jit(solution)/shard_map/while/body/eval_jaxpr/reduce_sum | solution.py:103
  192.5 11.3 %convert_reduce_fusion.2 = bf16[256,1024]{1,0:T(8,128)(2,1)S(1)} fusion(s32[1024,32]{0,1:T(8,128)S(1)} %get-tuple-element.201, s32[256]{0:T(256)S(1)} %iota_add_fusion.2), kind=kLoop, calls=%fused_computation.4.clone.1 | loop fusion | flops 24903680 | bytes 656384 | tf_op jit(solution)/shard_map/while/body/eval_jaxpr/reduce_sum | solution.py:103
  203.8 1.0 fusion.39
  206.1 11.3 %convert_reduce_fusion.2 = bf16[256,1024]{1,0:T(8,128)(2,1)S(1)} fusion(s32[1024,32]{0,1:T(8,128)S(1)} %get-tuple-element.201, s32[256]{0:T(256)S(1)} %iota_add_fusion.2), kind=kLoop, calls=%fused_computation.4.clone.1 | loop fusion | flops 24903680 | bytes 656384 | tf_op jit(solution)/shard_map/while/body/eval_jaxpr/reduce_sum | solution.py:103
  219.7 11.3 %convert_reduce_fusion.2 = bf16[256,1024]{1,0:T(8,128)(2,1)S(1)} fusion(s32[1024,32]{0,1:T(8,128)S(1)} %get-tuple-element.201, s32[256]{0:T(256)S(1)} %iota_add_fusion.2), kind=kLoop, calls=%fused_computation.4.clone.1 | loop fusion | flops 24903680 | bytes 656384 | tf_op jit(solution)/shard_map/while/body/eval_jaxpr/reduce_sum | solution.py:103
  233.3 11.3 %convert_reduce_fusion.2 = bf16[256,1024]{1,0:T(8,128)(2,1)S(1)} fusion(s32[1024,32]{0,1:T(8,128)S(1)} %get-tuple-element.201, s32[256]{0:T(256)S(1)} %iota_add_fusion.2), kind=kLoop, calls=%fused_computation.4.clone.1 | loop fusion | flops 24903680 | bytes 656384 | tf_op jit(solution)/shard_map/while/body/eval_jaxpr/reduce_sum | solution.py:103
  246.9 11.3 %convert_reduce_fusion.2 = bf16[256,1024]{1,0:T(8,128)(2,1)S(1)} fusion(s32[1024,32]{0,1:T(8,128)S(1)} %get-tuple-element.201, s32[256]{0:T(256)S(1)} %iota_add_fusion.2), kind=kLoop, calls=%fused_computation.4.clone.1 | loop fusion | flops 24903680 | bytes 656384 | tf_op jit(solution)/shard_map/while/body/eval_jaxpr/reduce_sum | solution.py:103
  258.2 1.0 fusion.39
  259.3 6.7 %all-to-all-start.1 = ((f32[16,256,256]{2,1,0:T(8,128)}), f32[16,256,256]{2,1,0:T(8,128)}, u32[]{:S(2)}, u32[]{:S(2)}) async-start(f32[16,256,256]{2,1,0:T(8,128)} %get-tuple-element.62), calls=%async_computation.1 | async-start | bytes 8388608 | tf_op jit(solution)/shard_map/all_to_all | solution.py:113
  266.0 51.8 %all-to-all-done.1 = f32[16,256,256]{2,1,0:T(8,128)} async-done(((f32[16,256,256]{2,1,0:T(8,128)}), f32[16,256,256]{2,1,0:T(8,128)}, u32[]{:S(2)}, u32[]{:S(2)}) %all-to-all-start.1) | async-done | bytes 4194336 | tf_op jit(solution)/shard_map/all_to_all | solution.py:113
  317.8 45.4 %while.23 = (s32[]{:T(128)}, f32[2048,256]{1,0:T(8,128)S(1)}, s32[16,256]{1,0:T(8,128)S(1)}, f32[16,256,256]{2,1,0:T(8,128)}, s32[]{:T(128)}, /*index=5*/s32[]{:T(128)}) while((s32[]{:T(128)}, f32[2048,256]{1,0:T(8,128)S(1)}, s32[16,256]{1,0:T(8,128)S(1)}, f32[16,256,256]{2,1,0:T(8,128)}, s32[]{:T(128)}, /*index=5*/s32[]{:T(128)}) %tuple.60), condition=%wide.region_6.7_spmd.clone, body=%wide.region_5.6_spmd.clone.sunk | while | flops 1612185600 | bytes 4460115 | solution.py:132
  317.8 2.8 convolution_add_fusion.2
  320.7 2.8 convolution_add_fusion.2
  323.5 2.8 convolution_add_fusion.2
  326.4 2.8 convolution_add_fusion.2
  329.2 2.8 convolution_add_fusion.2
  332.0 2.8 convolution_add_fusion.2
  334.9 2.8 convolution_add_fusion.2
  337.7 2.8 convolution_add_fusion.2
  340.6 2.8 convolution_add_fusion.2
  343.4 2.8 convolution_add_fusion.2
  346.2 2.8 convolution_add_fusion.2
  349.1 2.8 convolution_add_fusion.2
  351.9 2.8 convolution_add_fusion.2
  354.8 2.8 convolution_add_fusion.2
  357.6 2.8 convolution_add_fusion.2
  360.4 2.8 convolution_add_fusion.2
  363.2 1.7 collective-permute-start.2
  365.0 41.8 %collective-permute-done.2 = f32[2048,256]{1,0:T(8,128)S(1)} collective-permute-done((f32[2048,256]{1,0:T(8,128)S(1)}, f32[2048,256]{1,0:T(8,128)S(1)}, u32[]{:S(2)}, u32[]{:S(2)}) %collective-permute-start.2) | collective-permute-done | bytes 2097184 | tf_op jit(solution)/shard_map/ppermute | solution.py:19
  406.7 1.6 add.174
  408.3 3.0 collective-permute-start.3
  411.3 90.2 %collective-permute-done.3 = f32[2048,256]{1,0:T(8,128)} collective-permute-done((f32[2048,256]{1,0:T(8,128)}, f32[2048,256]{1,0:T(8,128)}, u32[]{:S(2)}, u32[]{:S(2)}) %collective-permute-start.3) | collective-permute-done | bytes 2097184 | tf_op jit(solution)/shard_map/ppermute | solution.py:19
  501.5 2.5 add.175
  504.0 6.7 %collective-permute-start.4 = (f32[2048,256]{1,0:T(8,128)S(1)}, f32[2048,256]{1,0:T(8,128)}, u32[]{:S(2)}, u32[]{:S(2)}) collective-permute-start(f32[2048,256]{1,0:T(8,128)S(1)} %add.175), channel_id=1, source_target_pairs={{0,8},{2,10},{4,12},{6,14},{8,0},{10,2},{12,4},{14,6},{1,9},{3,11}... | collective-permute-start | bytes 6291464 | tf_op jit(solution)/shard_map/ppermute | solution.py:19
  512.7 7.4 %collective-permute-start.5 = (f32[2,64]{1,0:T(2,128)S(1)}, f32[2,64]{1,0:T(2,128)S(1)}, u32[]{:S(2)}, u32[]{:S(2)}) collective-permute-start(f32[2,64]{1,0:T(2,128)S(1)} %pad_maximum_fusion.2), channel_id=1, source_target_pairs={{0,128},{128,0},{16,144},{144,16},{32,160},{160,32},{48,176},{176,... | collective-permute-start | bytes 1544 | tf_op jit(solution)/shard_map/ppermute | solution.py:37
  521.2 3.0 collective-permute-start
  524.4 2.5 collective-permute-done.1
  530.3 70.9 %collective-permute-done.4 = f32[2048,256]{1,0:T(8,128)} collective-permute-done((f32[2048,256]{1,0:T(8,128)S(1)}, f32[2048,256]{1,0:T(8,128)}, u32[]{:S(2)}, u32[]{:S(2)}) %collective-permute-start.4) | collective-permute-done | bytes 2097184 | tf_op jit(solution)/shard_map/ppermute | solution.py:19
  601.2 1.9 multiply_reduce_fusion
  603.2 3.8 psum.7
  607.6 5.5 divide_subtract_fusion
  (103 shorter events, 26.5 us)
Async XLA Ops:
  1.3 3.2 copy-start.3
  4.5 1.3 copy-start.4
  4.5 1.4 copy-start.5
  30.9 1.6 copy-start.1
  30.9 2.3 copy-start.6
  30.9 10.6 %copy-start = (bf16[1024,256]{1,0:T(8,128)(2,1)S(1)}, bf16[1024,256]{1,0:T(8,128)(2,1)}, u32[]{:S(2)}) copy-start(bf16[1024,256]{1,0:T(8,128)(2,1)} %param.16) | copy-start | bytes 1572868
  30.9 10.6 %copy-start.2 = (s32[1024,32]{0,1:T(8,128)S(1)}, s32[1024,32]{0,1:T(8,128)}, u32[]{:S(2)}) copy-start(s32[1024,32]{0,1:T(8,128)} %param.17) | copy-start | bytes 393220
  33.9 225.3 %all-to-all-start = ((s32[16,1,256]{2,1,0:T(1,128)}), s32[16,1,256]{2,1,0:T(1,128)S(1)}, u32[]{:S(2)}, u32[]{:S(2)}) async-start(s32[16,1,256]{2,1,0:T(1,128)} %copy.23), calls=%async_computation | async-start | bytes 32768 | tf_op jit(solution)/shard_map/all_to_all | solution.py:114
  259.3 58.6 %all-to-all-start.1 = ((f32[16,256,256]{2,1,0:T(8,128)}), f32[16,256,256]{2,1,0:T(8,128)}, u32[]{:S(2)}, u32[]{:S(2)}) async-start(f32[16,256,256]{2,1,0:T(8,128)} %get-tuple-element.62), calls=%async_computation.1 | async-start | bytes 8388608 | tf_op jit(solution)/shard_map/all_to_all | solution.py:113
  363.2 43.5 %collective-permute-start.2 = (f32[2048,256]{1,0:T(8,128)S(1)}, f32[2048,256]{1,0:T(8,128)S(1)}, u32[]{:S(2)}, u32[]{:S(2)}) collective-permute-start(f32[2048,256]{1,0:T(8,128)S(1)} %get-tuple-element.63), channel_id=1, source_target_pairs={{0,2},{2,0},{4,6},{6,4},{8,10},{10,8},{12,14},{14,12},{1,3},{3,1},... | collective-permute-start | bytes 6291464 | tf_op jit(solution)/shard_map/ppermute | solution.py:19
  408.3 93.2 %collective-permute-start.3 = (f32[2048,256]{1,0:T(8,128)}, f32[2048,256]{1,0:T(8,128)}, u32[]{:S(2)}, u32[]{:S(2)}) collective-permute-start(f32[2048,256]{1,0:T(8,128)} %add.174), channel_id=1, source_target_pairs={{0,4},{2,6},{4,0},{6,2},{8,12},{10,14},{12,8},{14,10},{1,5},{3,7},... | collective-permute-start | bytes 6291464 | tf_op jit(solution)/shard_map/ppermute | solution.py:19
  504.0 97.2 %collective-permute-start.4 = (f32[2048,256]{1,0:T(8,128)S(1)}, f32[2048,256]{1,0:T(8,128)}, u32[]{:S(2)}, u32[]{:S(2)}) collective-permute-start(f32[2048,256]{1,0:T(8,128)S(1)} %add.175), channel_id=1, source_target_pairs={{0,8},{2,10},{4,12},{6,14},{8,0},{10,2},{12,4},{14,6},{1,9},{3,11}... | collective-permute-start | bytes 6291464 | tf_op jit(solution)/shard_map/ppermute | solution.py:19
  512.7 11.5 %collective-permute-start.5 = (f32[2,64]{1,0:T(2,128)S(1)}, f32[2,64]{1,0:T(2,128)S(1)}, u32[]{:S(2)}, u32[]{:S(2)}) collective-permute-start(f32[2,64]{1,0:T(2,128)S(1)} %pad_maximum_fusion.2), channel_id=1, source_target_pairs={{0,128},{128,0},{16,144},{144,16},{32,160},{160,32},{48,176},{176,... | collective-permute-start | bytes 1544 | tf_op jit(solution)/shard_map/ppermute | solution.py:37
  521.1 5.8 collective-permute-start.1
  521.2 7.8 %collective-permute-start = (f32[2,64,256]{2,1,0:T(8,128)S(1)}, f32[2,64,256]{2,1,0:T(8,128)S(1)}, u32[]{:S(2)}, u32[]{:S(2)}) collective-permute-start(f32[2,64,256]{2,1,0:T(8,128)S(1)} %pad_maximum_fusion), channel_id=1, source_target_pairs={{0,128},{128,0},{16,144},{144,16},{32,160},{160,32},{48,176},{176,... | collective-permute-start | bytes 393224 | tf_op jit(solution)/shard_map/ppermute | solution.py:37
